TPU v7x, 32 devices: a whole 2x2x4 slice. The times are simulated.
32 devices in a mesh: layer: 4 (over x, core), feat: 4 (over z), par: 2 (over y).
Axes of the slice: x: 2, y: 2, z: 4, core: 2. Of those that a mesh axis runs over, the one named last changes fastest.
Arguments:
- residual: bfloat16 [4, 512, 2304], P('layer'), may hold values from -6 to 6
- norm_gain: float32 [4, 2304], P('layer'), may hold values from 0.5 to 1.5
- gate_weight: bfloat16 [4, 2304, 9216], P('layer', None, ('feat', 'par')), may hold values from -0.125 to 0.125
- up_weight: bfloat16 [4, 2304, 9216], P('layer', None, ('feat', 'par')), may hold values from -0.125 to 0.125
- down_weight: bfloat16 [4, 9216, 2304], P('layer', ('feat', 'par')), may hold values from -0.0625 to 0.0625
- enc_weight: float32 [4, 2304, 8192], P('layer', 'par', 'feat'), may hold values from -0.125 to 0.125
- enc_bias: float32 [4, 8192], P('layer', 'feat'), may hold values from -1 to 0.5
- dec_weight: bfloat16 [4, 2, 2, 8192, 2304], P('layer', 'par', None, 'feat'), may hold values from -0.0625 to 0.0625
- dec_bias: float32 [4, 2304], replicated, may hold values from -3 to 3
Outputs:
- enc_grad: float32 [4, 2304, 8192], P('layer', 'par', 'feat')
- enc_bias_grad: float32 [4, 8192], P('layer', 'feat')
- dec_grad: bfloat16 [4, 2, 2, 8192, 2304], P('layer', 'par', None, 'feat')
All inputs are finite; a program needn't handle non-finite values.
Results may differ from a plain program's by a relative error of at most 0.007.
Values may be sent and summed in bfloat16 or wider, within the bound.
No kernel may reach another device: no remote copies, remote signals or barrier semaphores. Data moves between devices by JAX's collectives and lax.ppermute only.
A program may use at most 192 MiB of HBM per device.

v0:
```python
import jax
import jax.numpy as jnp
from jax import lax
from jax.sharding import PartitionSpec as P


def partner_2(value, axis, stride):
    mask = 2**stride
    pairs = [(source, source ^ mask) for source in range(lax.axis_size(axis))]
    return lax.ppermute(value, axis, pairs)


def rms_normed(rows_in, gain_row):
    values = rows_in.astype(jnp.float32)
    scaling = lax.rsqrt(jnp.mean(values * values, axis=-1, keepdims=True) + 1e-06)
    return (values * scaling * gain_row).astype(jnp.bfloat16)


def shards(
    residual,
    norm_gain,
    gate_weight,
    up_weight,
    down_weight,
    enc_weight,
    enc_bias,
    dec_weight,
    dec_bias,
):
    highest = lax.Precision.HIGHEST
    source = lax.axis_index("layer")
    parity = lax.axis_index("par")
    slot_count = dec_weight.shape[2]
    normed = rms_normed(residual[0], norm_gain[0])
    tokens, model_width = normed.shape
    gate_value = jnp.dot(normed, gate_weight[0], preferred_element_type=jnp.float32)
    up_value = jnp.dot(normed, up_weight[0], preferred_element_type=jnp.float32)
    hidden = (jax.nn.gelu(gate_value, approximate=True) * up_value).astype(jnp.bfloat16)
    target_part = jnp.dot(hidden, down_weight[0], preferred_element_type=jnp.float32)
    half_width = enc_weight.shape[1]
    my_rows = lax.dynamic_slice_in_dim(normed, parity * half_width, half_width, 1).astype(
        jnp.float32
    )
    pre_part = jnp.dot(my_rows, enc_weight[0], precision=highest)
    pre_act = lax.psum(pre_part, "par") + enc_bias[0]
    positive = jnp.maximum(pre_act, 0.0)
    actives = (positive * positive).astype(jnp.bfloat16)
    slot_ids = jnp.arange(slot_count, dtype=jnp.int32)
    slot_live = 2 * slot_ids + parity >= source
    live_float = slot_live.astype(jnp.float32)
    decoders = dec_weight[0, 0]
    recon_parts = (
        jnp.einsum("tf,jfd->jtd", actives, decoders, preferred_element_type=jnp.float32)
        * live_float[:, None, None]
    )
    bias_slots = lax.dynamic_index_in_dim(
        dec_bias.reshape(slot_count, 2, model_width), parity, 1, keepdims=False
    )
    partner = partner_2(target_part, "par", 0)
    own_slot = ((slot_ids == source // 2) & (source % 2 == parity)).astype(jnp.float32)
    contrib = recon_parts - own_slot[:, None, None] * (target_part + partner)[None]
    summed_rows = lax.psum(contrib, ("layer", "feat"))
    err_full = summed_rows + bias_slots[:, None, :]
    errors = (err_full * 0.0625).astype(jnp.bfloat16)
    masked = errors * slot_live.astype(jnp.bfloat16)[:, None, None]
    back_part = jnp.einsum("jtd,jfd->tf", masked, decoders, preferred_element_type=jnp.float32)
    back_grad = lax.psum(back_part.astype(jnp.bfloat16), "par").astype(jnp.float32)
    d_pre = back_grad * 2.0 * positive
    enc_grad = lax.dot_general(my_rows, d_pre, (((0,), (0,)), ((), ())), precision=highest)
    bias_grad = jnp.sum(d_pre, axis=0)
    dec_grad = jnp.einsum(
        "tf,jtd->jfd", actives, masked, preferred_element_type=jnp.float32
    ).astype(jnp.bfloat16)
    return (enc_grad[None], bias_grad[None], dec_grad[None, None])


def solution(mesh):
    return jax.shard_map(
        shards,
        mesh=mesh,
        in_specs=(
            P("layer", None, None),
            P("layer", None),
            P("layer", None, ("feat", "par")),
            P("layer", None, ("feat", "par")),
            P("layer", ("feat", "par"), None),
            P("layer", "par", "feat"),
            P("layer", "feat"),
            P("layer", "par", None, "feat", None),
            P(),
        ),
        out_specs=(
            P("layer", "par", "feat"),
            P("layer", "feat"),
            P("layer", "par", None, "feat", None),
        ),
        check_vma=False,
    )
```

profile of v0, /device:TPU:0, one launch (start us, length us, event | category | flops | bytes accessed | tf_op | source)
XLA Modules:
  0.0 536.0 jit_solution(9293100787863199491)
XLA Ops:
  7.2 0.0 all-reduce.4.cloned.1.call-start
  7.2 2.2 multiply_reduce_fusion
  9.4 0.7 reduce
  10.2 0.0 copy-start
  10.2 8.3 %fusion.29 = f32[512,1152]{1,0:T(8,128)} fusion(bf16[1,2304,1152]{2,1,0:T(8,128)(2,1)} %param.11, bf16[1,512,2304]{2,1,0:T(8,128)(2,1)} %param.9, f32[2304]{0:T(1024)S(1)} %reduce, f32[512]{0:T(512)S(1)} %add_rsqrt_fusion), kind=kOutput, calls=%fused_computation.35 | convolution fusion | flops 2727346176 | bytes 10038272 | tf_op jit(solution)/shard_map/dot_general | solution.py:36
  18.4 0.0 copy-done
  18.4 13.4 %fusion.6 = f32[512,2304]{1,0:T(8,128)} fusion(bf16[1,1152,2304]{2,1,0:T(8,128)(2,1)} %param.13, f32[512,1152]{1,0:T(8,128)} %fusion.29, bf16[1,2304,1152]{2,1,0:T(8,128)(2,1)} %param.12, bf16[1,512,2304]{2,1,0:T(8,128)(2,1)S(1)} %copy-done, f32[2304]{0:T(1024)S(1)} %reduce, f32[512]{0:T(512)S(1)} %add_rsqrt_fusion), kind=kOutput, calls=%fused_computation.12 | convolution fusion | flops 5441716224 | bytes 20065280 | tf_op jit(solution)/shard_map/dot_general | solution.py:39
  31.8 3.0 collective-permute-start
  34.8 2.5 convert_bitcast_fusion.1
  37.3 0.1 dynamic-slice
  37.4 13.5 %fusion.4 = f32[512,2048]{1,0:T(8,128)} fusion(f32[1,1152,2048]{2,1,0:T(8,128)} %param.14, f32[512,2304]{1,0:T(8,128)} %convert_bitcast_fusion.1, s32[]{:T(128)S(6)} %select_n.18, f32[1152]{0:T(1024)S(1)} %dynamic-slice, f32[512]{0:T(512)S(1)} %add_rsqrt_fusion), kind=kOutput, calls=%fused_computation.6 | convolution fusion | flops 14497284096 | bytes 15997444 | tf_op jit(solution)/shard_map/dot_general | solution.py:44
  50.9 0.0 all-reduce.4.cloned.1.call-update
  50.9 0.0 all-reduce.6.cloned.1.call-start
  51.0 0.0 copy-start.4
  51.0 155.3 %collective-permute-done = f32[512,2304]{1,0:T(8,128)} collective-permute-done((f32[512,2304]{1,0:T(8,128)}, f32[512,2304]{1,0:T(8,128)}, u32[]{:S(2)}, u32[]{:S(2)}) %collective-permute-start) | collective-permute-done | bytes 4718624 | tf_op jit(solution)/shard_map/ppermute | solution.py:10
  206.3 6.5 %add.86 = f32[512,2304]{1,0:T(8,128)} add(f32[512,2304]{1,0:T(8,128)} %fusion.6, f32[512,2304]{1,0:T(8,128)} %collective-permute-done) | non-fusion elementwise | flops 1179648 | bytes 14155776 | tf_op jit(solution)/shard_map/add | solution.py:61
  212.8 14.1 %all-reduce.4.cloned.1.call-done = f32[512,2048]{1,0:T(8,128)} async-done(((f32[512,2048]{1,0:T(8,128)}), f32[512,2048]{1,0:T(8,128)}) %all-reduce.4.cloned.1.call-update) | async-done | bytes 4194320 | tf_op jit(solution)/shard_map/psum | solution.py:45
  226.9 0.0 copy-done.4
  226.9 18.0 %bitcast_subtract_fusion = f32[2,512,2304]{2,1,0:T(8,128)} fusion(f32[512,2304]{1,0:T(8,128)} %add.86, f32[2]{0:T(128)S(1)} %get-tuple-element.6, f32[2]{0:T(128)S(1)} %get-tuple-element.7, bf16[1,1,2,2048,2304]{4,3,2,1,0:T(8,128)(2,1)} %param.16, f32[512,2048]{1,0:T(8,128)} %all-reduce.4.cloned.1.call-done, f32[2048]{0:T(1024)S(1)} %bitcast.61), kind=kOutput, calls=%fused_computation.5 | convolution fusion | flops 9674948608 | bytes 37232656 | tf_op jit(solution)/shard_map/tf,jfd->jtd/dot_general | solution.py:53
  244.9 0.0 copy-start.3
  244.9 0.0 all-reduce.6.cloned.1.call-update
  245.0 0.0 all-reduce.8.cloned.1.call-start
  245.0 0.7 copy-done.3
  245.8 185.5 %all-reduce.6.cloned.1.call-done = f32[2,512,2304]{2,1,0:T(8,128)} async-done(((f32[2,512,2304]{2,1,0:T(8,128)}), f32[2,512,2304]{2,1,0:T(8,128)}) %all-reduce.6.cloned.1.call-update) | async-done | bytes 9437200 | tf_op jit(solution)/shard_map/psum | solution.py:62
  431.3 17.5 %bitcast_convert_fusion = bf16[512,2048]{1,0:T(8,128)(2,1)} fusion(bf16[1,1,2,2048,2304]{4,3,2,1,0:T(8,128)(2,1)} %param.16, f32[2,512,2304]{2,1,0:T(8,128)} %all-reduce.6.cloned.1.call-done, f32[2,2304]{1,0:T(2,128)S(1)} %bitcast.59, bf16[2]{0:T(256)(128)(2,1)S(1)} %compare_convert_fusion), kind=kOutput, calls=%fused_computation.22 | convolution fusion | flops 9674162176 | bytes 30427140 | tf_op jit(solution)/shard_map/jtd,jfd->tf/dot_general | solution.py:66
  448.8 0.0 all-reduce.8.cloned.1.call-update
  448.8 17.7 %convert_bitcast_fusion = bf16[1,1,2,2048,2304]{3,4,2,1,0:T(8,128)(2,1)} fusion(f32[512,2048]{1,0:T(8,128)} %all-reduce.4.cloned.1.call-done, f32[2048]{0:T(1024)S(1)} %bitcast.62, f32[2,512,2304]{2,1,0:T(8,128)} %all-reduce.6.cloned.1.call-done, f32[2,2304]{1,0:T(2,128)S(1)} %bitcast.60, bf16[2]{0:T(256)(128)(2,1)S(1)} %compare_convert_fusion), kind=kOutput, calls=%fused_computation.4 | convolution fusion | flops 9686745088 | bytes 32532484 | tf_op jit(solution)/shard_map/tf,jtd->jfd/dot_general | solution.py:71
  466.5 24.8 %copy.13 = bf16[1,1,2,2048,2304]{4,3,2,1,0:T(8,128)(2,1)} copy(bf16[1,1,2,2048,2304]{3,4,2,1,0:T(8,128)(2,1)} %convert_bitcast_fusion) | data formatting | bytes 37748736
  491.2 20.8 %all-reduce.8.cloned.1.call-done = bf16[512,2048]{1,0:T(8,128)(2,1)} async-done(((bf16[512,2048]{1,0:T(8,128)(2,1)}), bf16[512,2048]{1,0:T(8,128)(2,1)}) %all-reduce.8.cloned.1.call-update) | async-done | bytes 2097168 | tf_op jit(solution)/shard_map/psum | solution.py:67
  512.0 0.0 copy-start.1
  512.0 0.0 copy-start.2
  512.0 4.5 fusion.35
  516.5 0.0 copy-done.1
  516.5 0.3 copy-done.2
  516.7 12.7 %convolution_bitcast_fusion = f32[1,1152,2048]{2,1,0:T(8,128)} fusion(bf16[512,2048]{1,0:T(8,128)(2,1)S(1)} %copy-done.2, f32[512,2048]{1,0:T(8,128)S(1)} %copy-done.1, f32[2048]{0:T(1024)S(1)} %bitcast.64, f32[512,2304]{1,0:T(8,128)} %convert_bitcast_fusion.1, s32[]{:T(128)S(6)} %select_n.18, f32[1152]{0:T(1024)S(1)} %dynamic-slice, f32[512]{0:T(512)S(1)} %add_rsqrt_fusion), kind=kOutput, calls=%fused_computation.9 | convolution fusion | flops 14502526976 | bytes 18102788 | tf_op jit(solution)/shard_map/dot_general | solution.py:69
  (6 shorter events, 0.1 us)
Async XLA Ops:
  7.2 219.8 %all-reduce.4.cloned.1.call-start = ((), (), s32[]{:S(2)}) async-start(), calls=%async_computation | async-start | bytes 8388608 | tf_op jit(solution)/shard_map/psum | solution.py:45
  10.2 8.3 %copy-start = (bf16[1,512,2304]{2,1,0:T(8,128)(2,1)S(1)}, bf16[1,512,2304]{2,1,0:T(8,128)(2,1)}, u32[]{:S(2)}) copy-start(bf16[1,512,2304]{2,1,0:T(8,128)(2,1)} %param.9) | copy-start | bytes 7077892
  31.8 174.5 %collective-permute-start = (f32[512,2304]{1,0:T(8,128)}, f32[512,2304]{1,0:T(8,128)}, u32[]{:S(2)}, u32[]{:S(2)}) collective-permute-start(f32[512,2304]{1,0:T(8,128)} %fusion.6), channel_id=1, source_target_pairs={{0,1},{1,0},{2,3},{3,2},{4,5},{5,4},{6,7},{7,6},{8,9},{9,8},{10,11... | collective-permute-start | bytes 14155784 | tf_op jit(solution)/shard_map/ppermute | solution.py:10
  50.9 380.4 %all-reduce.6.cloned.1.call-start = ((), (), s32[]{:S(2)}) async-start(), calls=%async_computation.1 | async-start | bytes 18874368 | tf_op jit(solution)/shard_map/psum | solution.py:62
  51.0 176.0 %copy-start.4 = (f32[1,2048]{1,0:T(1,128)S(1)}, f32[1,2048]{1,0:T(1,128)}, u32[]{:S(2)}) copy-start(f32[1,2048]{1,0:T(1,128)} %param.15) | copy-start | bytes 24580
  244.9 0.8 copy-start.3
  245.0 267.1 %all-reduce.8.cloned.1.call-start = ((), (), s32[]{:S(2)}) async-start(), calls=%async_computation.2 | async-start | bytes 4194304 | tf_op jit(solution)/shard_map/psum | solution.py:67
  512.0 4.5 copy-start.1
  512.0 4.7 copy-start.2
Sparse Core Ops, SparseCore 0:
  51.0 175.8 all-reduce.3
  245.1 186.1 all-reduce.5
  448.9 63.0 all-reduce.7
where the time goes:
time: 537 us; the launch traced here: 536 us
  waiting for transfers between devices  376 us (70%)
  matrix products  101 us (19%)
  local copies, waits for them, and re-layouts  25.9 us (5%)
  other arithmetic  16.4 us (3%)
  between operations  13.8 us (3%)
    psum x1, waiting for transfers between devices, shards(): summed_rows = lax.psum(contrib, ('layer', 'feat'))  185 us
    ppermute x1, waiting for transfers between devices, partner_2(): return lax.ppermute(value, axis, pairs)  155 us
    unnamed x12, local copies, waits for them, and re-layouts  25.8 us
    psum x1, waiting for transfers between devices, shards(): lax.psum(back_part.astype(jnp.bfloat16), 'par').astype(jnp.float32)  20.8 us
    dot_general x1, matrix products, shards(): jnp.einsum('tf,jfd->jtd', actives, decoders, preferred_element_type=jnp.f...  18 us
    dot_general x1, matrix products, shards(): jnp.einsum('tf,jtd->jfd', actives, masked, preferred_element_type=jnp.flo...  17.7 us
    dot_general x1, matrix products, shards(): jnp.einsum('jtd,jfd->tf', masked, decoders, preferred_element_type=jnp.fl...  17.5 us
    psum x1, waiting for transfers between devices, shards(): pre_act = lax.psum(pre_part, 'par') + enc_bias[0]  14.1 us
  transfers between devices with their start and end apart: 4, of which 4 were waited for; matrix products, arithmetic and copies ran while one was open for 12% of the time, Pallas kernels for 0%

commit v1 on v0

--- a/solution.py
+++ b/solution.py
@@ -2,6 +2,7 @@
 import jax.numpy as jnp
 from jax import lax
 from jax.sharding import PartitionSpec as P
+from jax.lax import psum
 
 
 def partner_2(value, axis, stride):
@@ -59,7 +60,9 @@
     partner = partner_2(target_part, "par", 0)
     own_slot = ((slot_ids == source // 2) & (source % 2 == parity)).astype(jnp.float32)
     contrib = recon_parts - own_slot[:, None, None] * (target_part + partner)[None]
-    summed_rows = lax.psum(contrib, ("layer", "feat"))
+    summed_rows = contrib
+    for it in ("feat", "layer"):
+        summed_rows = psum(summed_rows, axis_name=it)
     err_full = summed_rows + bias_slots[:, None, :]
     errors = (err_full * 0.0625).astype(jnp.bfloat16)
     masked = errors * slot_live.astype(jnp.bfloat16)[:, None, None]

time: 537 us -> 848 us (1.58)
  waiting for transfers between devices: 376 us -> 687 us
    psum x1 -> x2, waiting for transfers between devices: 185 us -> 497 us  [shards(): summed_rows = psum(summed_rows, axis_name=it)]
  transfers between devices with their start and end apart: 4 -> 5, of which waited for: 4 -> 5; matrix products, arithmetic and copies ran while one was open for 12% -> 8% of each run, Pallas kernels for 0% -> 0%
where the time goes in v1:
time: 848 us; the launch traced here: 847 us
  waiting for transfers between devices  687 us (81%)
  matrix products  101 us (12%)
  local copies, waits for them, and re-layouts  25.9 us (3%)
  other arithmetic  16.4 us (2%)
  between operations  13.8 us (2%)
    psum x2, waiting for transfers between devices, shards(): summed_rows = psum(summed_rows, axis_name=it)  497 us
    ppermute x1, waiting for transfers between devices, partner_2(): return lax.ppermute(value, axis, pairs)  155 us
    unnamed x12, local copies, waits for them, and re-layouts  25.8 us
    psum x1, waiting for transfers between devices, shards(): lax.psum(back_part.astype(jnp.bfloat16), 'par').astype(jnp.float32)  20.9 us
    dot_general x1, matrix products, shards(): jnp.einsum('tf,jfd->jtd', actives, decoders, preferred_element_type=jnp.f...  18 us
    dot_general x1, matrix products, shards(): jnp.einsum('tf,jtd->jfd', actives, masked, preferred_element_type=jnp.flo...  17.7 us
    dot_general x1, matrix products, shards(): jnp.einsum('jtd,jfd->tf', masked, decoders, preferred_element_type=jnp.fl...  17.5 us
  transfers between devices with their start and end apart: 5, of which 5 were waited for; matrix products, arithmetic and copies ran while one was open for 8% of the time, Pallas kernels for 0%

profile of v1, /device:TPU:0, one launch (start us, length us, event | category | flops | bytes accessed | tf_op | source)
XLA Modules:
  0.0 847.4 jit_solution(15310483714877353855)
XLA Ops:
  7.2 0.0 all-reduce.5.cloned.1.call-start
  7.2 2.2 multiply_reduce_fusion
  9.4 0.7 reduce
  10.2 0.0 copy-start
  10.2 8.3 fusion.29
  18.4 0.0 copy-done
  18.4 13.4 %fusion.6 = f32[512,2304]{1,0:T(8,128)} fusion(bf16[1,1152,2304]{2,1,0:T(8,128)(2,1)} %param.13, f32[512,1152]{1,0:T(8,128)} %fusion.29, bf16[1,2304,1152]{2,1,0:T(8,128)(2,1)} %param.12, bf16[1,512,2304]{2,1,0:T(8,128)(2,1)S(1)} %copy-done, f32[2304]{0:T(1024)S(1)} %reduce, f32[512]{0:T(512)S(1)} %add_rsqrt_fusion), kind=kOutput, calls=%fused_computation.12 | convolution fusion | flops 5441716224 | bytes 20065280 | tf_op jit(solution)/shard_map/dot_general | solution.py:40
  31.8 3.0 collective-permute-start
  34.8 2.5 convert_bitcast_fusion.1
  37.3 0.1 dynamic-slice
  37.4 13.5 %fusion.4 = f32[512,2048]{1,0:T(8,128)} fusion(f32[1,1152,2048]{2,1,0:T(8,128)} %param.14, f32[512,2304]{1,0:T(8,128)} %convert_bitcast_fusion.1, s32[]{:T(128)S(6)} %select_n.18, f32[1152]{0:T(1024)S(1)} %dynamic-slice, f32[512]{0:T(512)S(1)} %add_rsqrt_fusion), kind=kOutput, calls=%fused_computation.6 | convolution fusion | flops 14497284096 | bytes 15997444 | tf_op jit(solution)/shard_map/dot_general | solution.py:45
  50.9 0.0 all-reduce.5.cloned.1.call-update
  50.9 0.0 all-reduce.7.cloned.1.call-start
  51.0 0.0 copy-start.4
  51.0 155.3 %collective-permute-done = f32[512,2304]{1,0:T(8,128)} collective-permute-done((f32[512,2304]{1,0:T(8,128)}, f32[512,2304]{1,0:T(8,128)}, u32[]{:S(2)}, u32[]{:S(2)}) %collective-permute-start) | collective-permute-done | bytes 4718624 | tf_op jit(solution)/shard_map/ppermute | solution.py:11
  206.3 6.5 add.88
  212.8 14.1 %all-reduce.5.cloned.1.call-done = f32[512,2048]{1,0:T(8,128)} async-done(((f32[512,2048]{1,0:T(8,128)}), f32[512,2048]{1,0:T(8,128)}) %all-reduce.5.cloned.1.call-update) | async-done | bytes 4194320 | tf_op jit(solution)/shard_map/psum | solution.py:46
  226.9 0.0 copy-done.4
  226.9 18.0 %bitcast_subtract_fusion = f32[2,512,2304]{2,1,0:T(8,128)} fusion(f32[512,2304]{1,0:T(8,128)} %add.88, f32[2]{0:T(128)S(1)} %get-tuple-element.6, f32[2]{0:T(128)S(1)} %get-tuple-element.7, bf16[1,1,2,2048,2304]{4,3,2,1,0:T(8,128)(2,1)} %param.16, f32[512,2048]{1,0:T(8,128)} %all-reduce.5.cloned.1.call-done, f32[2048]{0:T(1024)S(1)} %bitcast.61), kind=kOutput, calls=%fused_computation.5 | convolution fusion | flops 9674948608 | bytes 37232656 | tf_op jit(solution)/shard_map/tf,jfd->jtd/dot_general | solution.py:54
  244.9 0.0 all-reduce.7.cloned.1.call-update
  245.0 0.0 all-reduce.9.cloned.1.call-start
  245.0 326.2 %all-reduce.7.cloned.1.call-done = f32[2,512,2304]{2,1,0:T(8,128)} async-done(((f32[2,512,2304]{2,1,0:T(8,128)}), f32[2,512,2304]{2,1,0:T(8,128)}) %all-reduce.7.cloned.1.call-update) | async-done | bytes 9437200 | tf_op jit(solution)/shard_map/psum | solution.py:65
  571.2 0.0 copy-start.3
  571.2 0.0 all-reduce.9.cloned.1.call-update
  571.3 0.0 all-reduce.11.cloned.1.call-start
  571.3 0.7 copy-done.3
  572.1 170.4 %all-reduce.9.cloned.1.call-done = f32[2,512,2304]{2,1,0:T(8,128)} async-done(((f32[2,512,2304]{2,1,0:T(8,128)}), f32[2,512,2304]{2,1,0:T(8,128)}) %all-reduce.9.cloned.1.call-update) | async-done | bytes 9437200 | tf_op jit(solution)/shard_map/psum | solution.py:65
  742.5 17.5 %bitcast_convert_fusion = bf16[512,2048]{1,0:T(8,128)(2,1)} fusion(bf16[1,1,2,2048,2304]{4,3,2,1,0:T(8,128)(2,1)} %param.16, f32[2,512,2304]{2,1,0:T(8,128)} %all-reduce.9.cloned.1.call-done, f32[2,2304]{1,0:T(2,128)S(1)} %bitcast.59, bf16[2]{0:T(256)(128)(2,1)S(1)} %compare_convert_fusion), kind=kOutput, calls=%fused_computation.22 | convolution fusion | flops 9674162176 | bytes 30427140 | tf_op jit(solution)/shard_map/jtd,jfd->tf/dot_general | solution.py:69
  760.0 0.0 all-reduce.11.cloned.1.call-update
  760.1 17.7 %convert_bitcast_fusion = bf16[1,1,2,2048,2304]{3,4,2,1,0:T(8,128)(2,1)} fusion(f32[512,2048]{1,0:T(8,128)} %all-reduce.5.cloned.1.call-done, f32[2048]{0:T(1024)S(1)} %bitcast.62, f32[2,512,2304]{2,1,0:T(8,128)} %all-reduce.9.cloned.1.call-done, f32[2,2304]{1,0:T(2,128)S(1)} %bitcast.60, bf16[2]{0:T(256)(128)(2,1)S(1)} %compare_convert_fusion), kind=kOutput, calls=%fused_computation.4 | convolution fusion | flops 9686745088 | bytes 32532484 | tf_op jit(solution)/shard_map/tf,jtd->jfd/dot_general | solution.py:74
  777.7 24.8 %copy.13 = bf16[1,1,2,2048,2304]{4,3,2,1,0:T(8,128)(2,1)} copy(bf16[1,1,2,2048,2304]{3,4,2,1,0:T(8,128)(2,1)} %convert_bitcast_fusion) | data formatting | bytes 37748736
  802.5 20.9 %all-reduce.11.cloned.1.call-done = bf16[512,2048]{1,0:T(8,128)(2,1)} async-done(((bf16[512,2048]{1,0:T(8,128)(2,1)}), bf16[512,2048]{1,0:T(8,128)(2,1)}) %all-reduce.11.cloned.1.call-update) | async-done | bytes 2097168 | tf_op jit(solution)/shard_map/psum | solution.py:70
  823.4 0.0 copy-start.1
  823.4 0.0 copy-start.2
  823.4 4.5 fusion.35
  827.8 0.0 copy-done.1
  827.8 0.3 copy-done.2
  828.1 12.7 %convolution_bitcast_fusion = f32[1,1152,2048]{2,1,0:T(8,128)} fusion(bf16[512,2048]{1,0:T(8,128)(2,1)S(1)} %copy-done.2, f32[512,2048]{1,0:T(8,128)S(1)} %copy-done.1, f32[2048]{0:T(1024)S(1)} %bitcast.64, f32[512,2304]{1,0:T(8,128)} %convert_bitcast_fusion.1, s32[]{:T(128)S(6)} %select_n.18, f32[1152]{0:T(1024)S(1)} %dynamic-slice, f32[512]{0:T(512)S(1)} %add_rsqrt_fusion), kind=kOutput, calls=%fused_computation.9 | convolution fusion | flops 14502526976 | bytes 18102788 | tf_op jit(solution)/shard_map/dot_general | solution.py:72
  (6 shorter events, 0.1 us)
Async XLA Ops:
  7.2 219.8 %all-reduce.5.cloned.1.call-start = ((), (), s32[]{:S(2)}) async-start(), calls=%async_computation | async-start | bytes 8388608 | tf_op jit(solution)/shard_map/psum | solution.py:46
  10.2 8.3 copy-start
  31.8 174.5 %collective-permute-start = (f32[512,2304]{1,0:T(8,128)}, f32[512,2304]{1,0:T(8,128)}, u32[]{:S(2)}, u32[]{:S(2)}) collective-permute-start(f32[512,2304]{1,0:T(8,128)} %fusion.6), channel_id=1, source_target_pairs={{0,1},{1,0},{2,3},{3,2},{4,5},{5,4},{6,7},{7,6},{8,9},{9,8},{10,11... | collective-permute-start | bytes 14155784 | tf_op jit(solution)/shard_map/ppermute | solution.py:11
  50.9 520.4 %all-reduce.7.cloned.1.call-start = ((), (), s32[]{:S(2)}) async-start(), calls=%async_computation.1 | async-start | bytes 18874368 | tf_op jit(solution)/shard_map/psum | solution.py:65
  51.0 176.0 %copy-start.4 = (f32[1,2048]{1,0:T(1,128)S(1)}, f32[1,2048]{1,0:T(1,128)}, u32[]{:S(2)}) copy-start(f32[1,2048]{1,0:T(1,128)} %param.15) | copy-start | bytes 24580
  245.0 497.6 %all-reduce.9.cloned.1.call-start = ((), (), s32[]{:S(2)}) async-start(), calls=%async_computation.2 | async-start | bytes 18874368 | tf_op jit(solution)/shard_map/psum | solution.py:65
  571.2 0.8 copy-start.3
  571.3 252.1 %all-reduce.11.cloned.1.call-start = ((), (), s32[]{:S(2)}) async-start(), calls=%async_computation.3 | async-start | bytes 4194304 | tf_op jit(solution)/shard_map/psum | solution.py:70
  823.4 4.5 copy-start.1
  823.4 4.7 copy-start.2
Sparse Core Ops, SparseCore 0:
  51.0 175.8 all-reduce.4
  245.1 326.1 all-reduce.6
  573.7 168.7 all-reduce.8
  760.2 63.1 all-reduce.10
